TPU v7x, 32 devices: a whole 2x2x4 slice. The times are simulated.
32 devices in a mesh: slides: 2 (over y), seq: 16 (over z, x, core), mp: 1.
Axes of the slice: x: 2, y: 2, z: 4, core: 2. Of those that a mesh axis runs over, the one named last changes fastest.
Arguments:
- tokens: bfloat16 [32768, 768], P(('slides', 'seq', 'mp')), parts along dimension 0, may hold values from -6 to 6
- attn_gain: float32 [768], replicated, may hold values from 0.25 to 1.75
- query_first: bfloat16 [768, 768], P(None, 'mp'), may hold values from -4 to 4
- key_first: bfloat16 [768, 768], P(None, 'mp'), may hold values from -4 to 4
- segment_value: bfloat16 [768, 768], P(None, 'mp'), may hold values from -0.21875 to 0.21875
- output_first: bfloat16 [768, 768], P('mp'), may hold values from -0.875 to 0.875
- mlp_gain: float32 [768], replicated, may hold values from 0.25 to 1.75
- up_weight: bfloat16 [768, 3072], P(None, 'mp'), may hold values from -0.21875 to 0.21875
- down_weight: bfloat16 [3072, 768], P('mp'), may hold values from -0.109375 to 0.109375
- second_gain: float32 [768], replicated, may hold values from 0.25 to 1.75
- query_second: bfloat16 [768, 768], P(None, 'mp'), may hold values from -4 to 4
- key_second: bfloat16 [768, 768], P(None, 'mp'), may hold values from -4 to 4
- value_second: bfloat16 [768, 768], P(None, 'mp'), may hold values from -0.21875 to 0.21875
- output_second: bfloat16 [768, 768], P('mp'), may hold values from -0.875 to 0.875
- segment_offset: int32 [16], P('mp'), may hold values from 0 to 63
- global_offset: int32 [16], P('mp'), may hold values from 0 to 63
Outputs:
- encoded: bfloat16 [32768, 768], P(('slides', 'seq', 'mp')), parts along dimension 0
There are 2 independent parts, one for each index of `slides`. A program takes and returns all parts, laid end to end along the dimension named above; an argument that names none is the same for every part. Nothing has to cross between parts.
All inputs are finite; a program needn't handle non-finite values.
Results may differ from a plain program's by a relative error of at most 0.03.
The roundings to bfloat16 on the way count: a program that leaves them out, or rounds other values in their place, can miss the bound.
Values may be sent and summed in bfloat16 or wider, within the bound.
A program may use at most 128 MiB of HBM per device.

v0:
```python
import functools
import math

import jax
import jax.numpy as jnp
from jax import lax
from jax.experimental import pallas as pl
from jax.experimental.pallas import tpu as pltpu
from jax.sharding import PartitionSpec as P

KEYS = 256
SEG_MAX = 16


def swapped(x, axis, apart):
    return lax.ppermute(x, axis, [(i, i ^ 1 << apart) for i in range(lax.axis_size(axis))])


def norm_rows(values, gain):
    center = values - jnp.mean(values, axis=-1, keepdims=True)
    spread = jnp.mean(center * center, axis=-1, keepdims=True)
    return (center * lax.rsqrt(spread + 1e-05) * gain).astype(jnp.bfloat16)


def pick_keys(hidden, offsets, stride, key_weight, value_weight):
    token_count, width = hidden.shape
    head_count = offsets.shape[0]
    head_size = key_weight.shape[1] // head_count
    grouped_rows = hidden.reshape(token_count // stride, stride, width)
    dilation_selector = (
        lax.broadcasted_iota(jnp.int32, (stride, head_count), 0) == offsets[None, :]
    ).astype(jnp.bfloat16)
    chosen = jnp.einsum(
        "nof,oj->njf", grouped_rows, dilation_selector, preferred_element_type=jnp.float32
    ).astype(jnp.bfloat16)
    key_heads = jnp.einsum(
        "xkr,rkf->xkf",
        chosen,
        key_weight.reshape(width, head_count, head_size),
        preferred_element_type=jnp.float32,
    ).astype(jnp.bfloat16)
    value_heads = jnp.einsum(
        "xkr,rkf->xkf",
        chosen,
        value_weight.reshape(width, head_count, head_size),
        preferred_element_type=jnp.float32,
    ).astype(jnp.bfloat16)
    picked = token_count // stride
    return jnp.stack(
        [
            key_heads.reshape(picked, head_count * head_size),
            value_heads.reshape(picked, head_count * head_size),
        ]
    )


def attend_local(query, keyval, head_count):
    token_count, width = query.shape
    head_size = width // head_count
    query_heads = query.reshape(token_count, head_count, head_size)
    key_heads = keyval[0].reshape(-1, head_count, head_size)
    value_heads = keyval[1].reshape(-1, head_count, head_size)
    scores = jnp.einsum(
        "thd,khd->htk", query_heads, key_heads, preferred_element_type=jnp.float32
    ) * head_size ** (-0.5)
    highest = jnp.max(scores, axis=-1, keepdims=True)
    weights = jnp.exp(scores - highest)
    weights = (weights / jnp.sum(weights, axis=-1, keepdims=True)).astype(jnp.bfloat16)
    mixed = jnp.einsum(
        "htk,khd->thd", weights, value_heads, preferred_element_type=jnp.float32
    ).astype(jnp.bfloat16)
    return mixed.reshape(token_count, width)


def merge_branch_pair(mine, other, level, token_position):
    lower = token_position >> level & 1 == 0
    return jnp.where(
        lower, jnp.concatenate((mine, other), axis=1), jnp.concatenate((other, mine), axis=1)
    )


def spread_segment(keyval, seg_span, token_position):
    for level in range(seg_span.bit_length() - 1):
        partner = swapped(keyval, "seq", level)
        keyval = merge_branch_pair(keyval, partner, level, token_position)
    return keyval


def spread_global(keyval_two):
    keyval_two = lax.all_gather(keyval_two, "seq", axis=1, tiled=True)
    return keyval_two


def combine(partial_value, residual_full, need_full):
    row_count = residual_full.shape[0] // lax.axis_size("mp")
    row_start = lax.axis_index("mp") * row_count
    share = lax.psum_scatter(partial_value, "mp", scatter_dimension=0, tiled=True)
    own_rows = lax.dynamic_slice_in_dim(residual_full, row_start, row_count, 0)
    own_rows = (own_rows.astype(jnp.float32) + share).astype(jnp.bfloat16)
    full_rows = lax.all_gather(own_rows, "mp", axis=0, tiled=True) if need_full else own_rows
    return (own_rows, full_rows)


def body(
    tokens,
    attn_gain,
    query_first,
    key_first,
    segment_value,
    output_first,
    mlp_gain,
    up_weight,
    down_weight,
    second_gain,
    query_second,
    key_second,
    value_second,
    output_second,
    segment_offset,
    global_offset,
):
    seq_count = lax.axis_size("seq")
    token_position = lax.axis_index("seq")
    seg_span = min(SEG_MAX, seq_count)
    head_count = segment_offset.shape[0]
    full_rows = lax.all_gather(tokens, "mp", axis=0, tiled=True)
    token_count = full_rows.shape[0]
    hidden = norm_rows(full_rows.astype(jnp.float32), attn_gain)
    query = jnp.dot(hidden, query_first, preferred_element_type=jnp.float32).astype(jnp.bfloat16)
    seg_stride = token_count // (KEYS // seg_span)
    keyval = pick_keys(hidden, segment_offset, seg_stride, key_first, segment_value)
    keyval = spread_segment(keyval, seg_span, token_position)
    mixed = attend_local(query, keyval, head_count)
    partial_value = jnp.dot(mixed, output_first, preferred_element_type=jnp.float32)
    own_rows, first_rows = combine(partial_value, full_rows, True)
    normed = norm_rows(first_rows.astype(jnp.float32), mlp_gain)
    inner = jax.nn.gelu(
        jnp.dot(normed, up_weight, preferred_element_type=jnp.float32), approximate=True
    ).astype(jnp.bfloat16)
    partial_value = jnp.dot(inner, down_weight, preferred_element_type=jnp.float32)
    own_rows, second_rows = combine(partial_value, first_rows, True)
    hidden_two = norm_rows(second_rows.astype(jnp.float32), second_gain)
    query_two = jnp.dot(hidden_two, query_second, preferred_element_type=jnp.float32).astype(
        jnp.bfloat16
    )
    glob_stride = token_count // (KEYS // seq_count)
    keyval_two = pick_keys(hidden_two, global_offset, glob_stride, key_second, value_second)
    keyval_two = spread_global(keyval_two)
    mixed_two = attend_local(query_two, keyval_two, head_count)
    partial_value = jnp.dot(mixed_two, output_second, preferred_element_type=jnp.float32)
    own_rows, unused_rows = combine(partial_value, second_rows, False)
    return own_rows


MESH = pl.DeviceIdType.MESH
F32 = jnp.float32
BF16 = jnp.bfloat16
WINDOW = 256
LANES = 128


def iota(shape, axis):
    return lax.broadcasted_iota(jnp.int32, shape, axis)


def dot32(a, b):
    return jnp.dot(a, b, preferred_element_type=F32)


def gelu(x):
    return 0.5 * x * (1.0 + jnp.tanh(math.sqrt(2.0 / math.pi) * (x + 0.044715 * (x * x * x))))


class Gather:
    def __init__(self, n, buf, ssem, rsem):
        me = lax.axis_index("seq")
        self.me, self.n, self.high = me, n, n // 4
        self.buf, self.ssem, self.rsem = buf, ssem, rsem
        self.b0, self.b1, self.hi = me % 2, (me // 2) % 2, me // 4
        self.peer1 = self.hi * 4 + (1 - self.b1) * 2 + self.b0
        self.peer0 = self.hi * 4 + self.b1 * 2 + (1 - self.b0)

    def slot(self, d, b1, b0):
        return ((self.hi + self.high - d) % self.high) * 4 + b1 * 2 + b0

    def copy(self, slot, peer, k):
        return pltpu.make_async_remote_copy(
            src_ref=self.buf.at[slot],
            dst_ref=self.buf.at[slot],
            send_sem=self.ssem.at[k],
            recv_sem=self.rsem.at[slot],
            device_id={"seq": peer},
            device_id_type=MESH,
        )

    def peers(self):
        out = [((self.hi + d) % self.high) * 4 + self.b1 * 2 + self.b0 for d in range(1, self.high)]
        return out + [self.peer1, self.peer0]

    def start(self):
        h = self.high
        for d in range(1, h):
            peer = ((self.hi + d) % h) * 4 + self.b1 * 2 + self.b0
            self.copy(self.me, peer, d - 1).start()
        self.copy(self.me, self.peer1, h - 1).start()
        self.copy(self.me, self.peer0, 2 * h - 1).start()

    def second(self):
        h = self.high
        for d in range(1, h):
            slot = self.slot(d, self.b1, self.b0)
            self.copy(slot, self.peer1, h - 1 + d).wait_recv()
            self.copy(slot, self.peer1, h - 1 + d).start()
            self.copy(slot, self.peer0, 2 * h - 1 + d).start()

    def third(self):
        h = self.high
        for d in range(h):
            slot = self.slot(d, 1 - self.b1, self.b0)
            self.copy(slot, self.peer0, 3 * h - 1 + d).wait_recv()
            self.copy(slot, self.peer0, 3 * h - 1 + d).start()

    def finish(self):
        h = self.high
        for b1 in (self.b1, 1 - self.b1):
            for d in range(h):
                slot = self.slot(d, b1, 1 - self.b0)
                self.copy(slot, self.peer0, 0).wait_recv()
        for k in range(4 * h - 1):
            self.copy(self.me, self.peer0, k).wait_send()


def head_column(offset_ref, heads, picked):
    rows = iota((heads * picked, 1), 0) // picked
    column = jnp.zeros((heads * picked, 1), jnp.int32)
    for h in range(heads):
        column = jnp.where(rows == h, offset_ref[h], column)
    return column


def kernel(
    n, heads, picked, stride,
    seg_ref, glob_ref, x_ref, gain1_ref, gain_mlp_ref, gain2_ref,
    wq1_hbm, wk1_hbm, wv1_hbm, wo1_hbm, up_hbm, down_hbm, wq2_hbm, wk2_hbm, wv2_hbm, wo2_hbm,
    out_ref,
    wq1, wk1, wv1, wo1, up, down, wq2, wk2, wv2, wo2, wo_pad1, wo_pad2,
    xp, q, kv1, kv2, km, vp, perm, perm_back, mix, inner, sem, ssem1, rsem1, ssem2, rsem2,
):
    tokens, width = x_ref.shape
    size = width // heads
    half = LANES // 2
    chunk = heads * picked
    chunks = tokens // chunk
    keys = n * picked
    group = WINDOW // stride
    scale = size ** -0.5 * math.log2(math.e)

    pairs = [(wk1_hbm, wk1), (wv1_hbm, wv1), (wq1_hbm, wq1), (wo1_hbm, wo1), (up_hbm, up),
             (down_hbm, down), (wk2_hbm, wk2), (wv2_hbm, wv2), (wq2_hbm, wq2), (wo2_hbm, wo2)]
    loads = [pltpu.make_async_copy(a, b, sem.at[i]) for i, (a, b) in enumerate(pairs)]
    for load in loads:
        load.start()

    first_gather = Gather(n, kv1, ssem1, rsem1)
    second_gather = Gather(n, kv2, ssem2, rsem2)
    barrier = pltpu.get_barrier_semaphore()
    peers = first_gather.peers()
    for peer in peers:
        pl.semaphore_signal(barrier, inc=1, device_id={"seq": peer}, device_id_type=MESH)

    def own_heads(hidden, weight):
        full = dot32(hidden, weight[...])
        column = iota((picked, width), 1)
        total = jnp.zeros((picked, width), F32)
        for h in range(heads):
            mine = (column >= h * size) & (column < h * size + size)
            total = jnp.where(mine, full[h * picked:(h + 1) * picked], total)
        return total.astype(BF16)

    rows = iota((chunk, 1), 0)
    pick = rows % picked
    target = pick * stride + head_column(seg_ref, heads, picked)
    onehot = (iota((chunk, tokens), 1) == target).astype(F32).astype(BF16)
    hidden = norm_rows(dot32(onehot, x_ref[...]), gain1_ref[...][None, :])
    me = first_gather.me
    loads[0].wait()
    kv1[me, 0:picked, :] = own_heads(hidden, wk1)
    loads[1].wait()
    kv1[me, picked:2 * picked, :] = own_heads(hidden, wv1)
    pl.semaphore_wait(barrier, len(peers))
    first_gather.start()

    glob_col = head_column(glob_ref, heads, picked)
    lane = iota((16, WINDOW), 1)
    inside = lane % stride
    chosen = jnp.zeros((16, WINDOW), F32)
    for h in range(heads):
        chosen = jnp.where(inside == glob_ref[h], 1.0, chosen)
    a, b = iota((WINDOW, WINDOW), 0), iota((WINDOW, WINDOW), 1)
    same = a // stride == b // stride
    before = jnp.where(same & (a < b), 1.0, 0.0).astype(BF16)
    count = dot32(chosen.astype(BF16), before)
    total = dot32(chosen.astype(BF16), jnp.where(same, 1.0, 0.0).astype(BF16))
    rank = jnp.where(chosen > 0.5, count, total + inside.astype(F32) - count)
    rank_row = rank[0:1, :]
    table = jnp.where(same & (rank_row == (a % stride).astype(F32)), 1.0, 0.0)
    perm[...] = table.astype(BF16)
    perm_back[...] = table.T.astype(BF16)
    at_head = (iota((chunk, WINDOW), 1) == glob_col)
    head_rank = jnp.sum(jnp.where(at_head, rank_row, 0.0), axis=1, keepdims=True)
    spot = (pick * heads).astype(F32) + head_rank
    onehot_two = (iota((chunk, chunk), 1).astype(F32) == spot).astype(F32).astype(BF16)

    for g in range(tokens // WINDOW):
        moved = dot32(perm[...], x_ref[g * WINDOW:(g + 1) * WINDOW, :]).astype(BF16)
        for j in range(group):
            for c in range(chunks):
                at = c * chunk + (g * group + j) * heads
                xp[at:at + heads, :] = moved[j * stride + c * heads:j * stride + (c + 1) * heads]

    def window_of(h):
        return min(h * size // LANES * LANES, width - WINDOW)

    for h in range(heads):
        km[h] = jnp.zeros((WINDOW, keys), BF16)
        i = h % 2
        ones = iota((keys, LANES), 1) // half == i
        vp[h // 2, i * keys:(i + 1) * keys, LANES:] = jnp.where(ones, 1.0, 0.0).astype(BF16)
    for source, padded, load in ((wo1, wo_pad1, loads[3]), (wo2, wo_pad2, None)):
        if load is None:
            continue
        load.wait()
        for h in range(heads):
            padded[h * half:h * half + size, :] = source[h * size:(h + 1) * size, :]
            padded[h * half + size:(h + 1) * half, :] = jnp.zeros((half - size, width), BF16)

    first_gather.second()

    loads[2].wait()

    def query_chunk(c, carry):
        at = pl.ds(pl.multiple_of(c * chunk, chunk), chunk)
        hidden = norm_rows(xp[at, :].astype(F32), gain1_ref[...][None, :])
        q[at, :] = dot32(hidden, wq1[...]).astype(BF16)
        return carry

    lax.fori_loop(0, chunks, query_chunk, 0)
    first_gather.third()
    first_gather.finish()

    def set_keys(kv):
        key = kv[:, 0:picked, :].reshape(keys, width)
        value = kv[:, picked:2 * picked, :].reshape(keys, width)
        turned = key.astype(F32).T.astype(BF16)
        for h in range(heads):
            begin = h * size - window_of(h)
            km[h, begin:begin + size, :] = turned[h * size:(h + 1) * size, :]
            i = h % 2
            c, l = iota((WINDOW, LANES), 0) - begin, iota((WINDOW, LANES), 1) - i * half
            shift = jnp.where((c == l) & (l >= 0) & (l < size), 1.0, 0.0).astype(BF16)
            moved = dot32(value[:, window_of(h):window_of(h) + WINDOW], shift)
            vp[h // 2, i * keys:(i + 1) * keys, 0:LANES] = moved.astype(BF16)

    def attend(at):
        for pair in range(heads // 2):
            parts = []
            for h in (2 * pair, 2 * pair + 1):
                start = window_of(h)
                scores = dot32(q[at, start:start + WINDOW], km[h])
                top = jnp.max(scores, axis=-1, keepdims=True)
                parts.append(jnp.exp2((scores - top) * scale).astype(BF16))
            both = dot32(jnp.concatenate(parts, axis=1), vp[pair])
            mixed = both[:, :LANES] / both[:, LANES:]
            mix[:, pair * LANES:(pair + 1) * LANES] = mixed.astype(BF16)

    set_keys(kv1)
    loads[4].wait()
    loads[5].wait()
    loads[6].wait()
    loads[7].wait()
    loads[8].wait()

    def first_chunk(c, carry):
        at = pl.ds(pl.multiple_of(c * chunk, chunk), chunk)
        attend(at)
        first = (xp[at, :].astype(F32) + dot32(mix[...], wo_pad1[...])).astype(BF16)
        normed = norm_rows(first.astype(F32), gain_mlp_ref[...][None, :])
        hidden_units = up.shape[1]
        for start in range(0, hidden_units, width):
            part = dot32(normed, up[:, start:start + width])
            inner[:, start:start + width] = gelu(part).astype(BF16)
        second = (first.astype(F32) + dot32(inner[...], down[...])).astype(BF16)
        xp[at, :] = second
        hidden_two = norm_rows(second.astype(F32), gain2_ref[...][None, :])
        q[at, :] = dot32(hidden_two, wq2[...]).astype(BF16)

        @pl.when(c == 0)
        def _():
            picked_rows = dot32(onehot_two, hidden_two).astype(BF16)
            kv2[me, 0:picked, :] = own_heads(picked_rows, wk2)
            kv2[me, picked:2 * picked, :] = own_heads(picked_rows, wv2)
            second_gather.start()

        @pl.when(c == 1)
        def _():
            second_gather.second()

        @pl.when(c == 2)
        def _():
            second_gather.third()

        return carry

    lax.fori_loop(0, chunks, first_chunk, 0)
    loads[9].wait()
    for h in range(heads):
        wo_pad2[h * half:h * half + size, :] = wo2[h * size:(h + 1) * size, :]
        wo_pad2[h * half + size:(h + 1) * half, :] = jnp.zeros((half - size, width), BF16)
    second_gather.finish()
    set_keys(kv2)

    def last_chunk(c, carry):
        at = pl.ds(pl.multiple_of(c * chunk, chunk), chunk)
        attend(at)
        xp[at, :] = (xp[at, :].astype(F32) + dot32(mix[...], wo_pad2[...])).astype(BF16)
        return carry

    lax.fori_loop(0, chunks, last_chunk, 0)
    for g in range(tokens // WINDOW):
        blocks = []
        for j in range(group):
            for c in range(chunks):
                at = c * chunk + (g * group + j) * heads
                blocks.append(xp[at:at + heads, :])
        moved = dot32(perm_back[...], jnp.concatenate(blocks, axis=0))
        out_ref[g * WINDOW:(g + 1) * WINDOW, :] = moved.astype(BF16)


def whole_body(
    tokens, attn_gain, query_first, key_first, segment_value, output_first, mlp_gain, up_weight,
    down_weight, second_gain, query_second, key_second, value_second, output_second,
    segment_offset, global_offset,
):
    n = lax.axis_size("seq")
    heads = segment_offset.shape[0]
    picked = KEYS // n
    count, width = tokens.shape
    stride = count // picked
    units = up_weight.shape[1]
    chunk = heads * picked
    any_space = pl.BlockSpec(memory_space=pl.ANY)
    vmem = pl.BlockSpec(memory_space=pltpu.VMEM)
    smem = pl.BlockSpec(memory_space=pltpu.SMEM)
    square = pltpu.VMEM((width, width), BF16)
    padded = pltpu.VMEM((heads * LANES // 2, width), BF16)
    return pl.pallas_call(
        functools.partial(kernel, n, heads, picked, stride),
        out_shape=jax.ShapeDtypeStruct(tokens.shape, tokens.dtype),
        in_specs=[smem, smem, vmem, vmem, vmem, vmem] + [any_space] * 10,
        out_specs=vmem,
        scratch_shapes=[
            square, square, square, square,
            pltpu.VMEM((width, units), BF16), pltpu.VMEM((units, width), BF16),
            square, square, square, square, padded, padded,
            pltpu.VMEM((count, width), BF16),
            pltpu.VMEM((count, width), BF16),
            pltpu.VMEM((n, 2 * picked, width), BF16),
            pltpu.VMEM((n, 2 * picked, width), BF16),
            pltpu.VMEM((heads, WINDOW, KEYS), BF16),
            pltpu.VMEM((heads // 2, 2 * KEYS, 2 * LANES), BF16),
            pltpu.VMEM((WINDOW, WINDOW), BF16),
            pltpu.VMEM((WINDOW, WINDOW), BF16),
            pltpu.VMEM((chunk, heads * LANES // 2), BF16),
            pltpu.VMEM((chunk, units), BF16),
            pltpu.SemaphoreType.DMA((10,)),
            pltpu.SemaphoreType.DMA((n,)), pltpu.SemaphoreType.DMA((n,)),
            pltpu.SemaphoreType.DMA((n,)), pltpu.SemaphoreType.DMA((n,)),
        ],
        compiler_params=pltpu.CompilerParams(
            collective_id=0, has_side_effects=True, vmem_limit_bytes=60 << 20
        ),
        name="encoder",
    )(
        segment_offset, global_offset, tokens, attn_gain, mlp_gain, second_gain,
        query_first, key_first, segment_value, output_first, up_weight, down_weight,
        query_second, key_second, value_second, output_second,
    )


def fits(mesh):
    n = mesh.shape["seq"]
    return mesh.shape["mp"] == 1 and n == SEG_MAX


def choose(mesh):
    return whole_body if fits(mesh) else body


def solution(mesh):
    placed = (
        P(("slides", "seq", "mp"), None),
        P(),
        P(None, "mp"),
        P(None, "mp"),
        P(None, "mp"),
        P("mp", None),
        P(),
        P(None, "mp"),
        P("mp", None),
        P(),
        P(None, "mp"),
        P(None, "mp"),
        P(None, "mp"),
        P("mp", None),
        P("mp"),
        P("mp"),
    )
    return jax.shard_map(
        choose(mesh),
        mesh=mesh,
        in_specs=placed,
        out_specs=P(("slides", "seq", "mp"), None),
        check_vma=False,
    )
```

profile of v0, /device:TPU:0, one launch (start us, length us, event | category | flops | bytes accessed | tf_op | source)
XLA Modules:
  0.0 57.0 jit_solution(13653587115485227200)
XLA Ops:
  0.0 54.4 %encoder.1 = bf16[1024,768]{1,0:T(8,128)(2,1)} custom-call(s32[16]{0:T(128)} %seg_ref.1, s32[16]{0:T(128)} %glob_ref.1, bf16[1024,768]{1,0:T(8,128)(2,1)} %x_ref.1, f32[768]{0:T(1024)} %gain1_ref.1, f32[768]{0:T(1024)} %gain_mlp_ref.1, f32[768]{0:T(1024)} %gain2_ref.1, bf16[768,768]{1,0:T(8,128)(2,1)} %wq1_hbm.1, bf16[768,768]{1,0:T(8,128)(2,1)} %wk1_hbm.1, ...), custom_call_target="tpu_custom_call" | custom-call | tf_op jit(solution)/shard_map/encoder/pallas_call | solution.py:456
  54.4 2.7 %copy.18 = bf16[1024,768]{1,0:T(8,128)(2,1)} copy(bf16[1024,768]{1,0:T(8,128)(2,1)} %encoder.1) | data formatting | bytes 3145728
where the time goes:
time: 57.2 us; the launch traced here: 57 us
  Pallas kernels  54.4 us (95%)
  local copies, waits for them, and re-layouts  2.65 us (5%)
    pallas_call x1, Pallas kernels, whole_body(): pl.pallas_call(functools.partial(kernel, n, heads, picked, stride), out_s...  54.4 us
    unnamed x1, local copies, waits for them, and re-layouts  2.65 us

commit v1 on v0

--- a/solution.py
+++ b/solution.py
@@ -157,6 +157,7 @@
 BF16 = jnp.bfloat16
 WINDOW = 256
 LANES = 128
+GROUP = 2
 
 
 def iota(shape, axis):
@@ -167,8 +168,19 @@
     return jnp.dot(a, b, preferred_element_type=F32)
 
 
+def dot_last(a, b):
+    return lax.dot_general(a, b, (((1,), (1,)), ((), ())), preferred_element_type=F32)
+
+
+def dot_first(a, b):
+    return lax.dot_general(a, b, (((0,), (0,)), ((), ())), preferred_element_type=F32)
+
+
 def gelu(x):
-    return 0.5 * x * (1.0 + jnp.tanh(math.sqrt(2.0 / math.pi) * (x + 0.044715 * (x * x * x))))
+    slope = math.sqrt(2.0 / math.pi)
+    bend = jnp.tanh(x * (x * x * (0.044715 * slope) + slope))
+    half = 0.5 * x
+    return half * bend + half
 
 
 class Gather:
@@ -205,20 +217,17 @@
         self.copy(self.me, self.peer1, h - 1).start()
         self.copy(self.me, self.peer0, 2 * h - 1).start()
 
-    def second(self):
+    def second(self, d):
         h = self.high
-        for d in range(1, h):
-            slot = self.slot(d, self.b1, self.b0)
-            self.copy(slot, self.peer1, h - 1 + d).wait_recv()
-            self.copy(slot, self.peer1, h - 1 + d).start()
-            self.copy(slot, self.peer0, 2 * h - 1 + d).start()
-
-    def third(self):
-        h = self.high
-        for d in range(h):
-            slot = self.slot(d, 1 - self.b1, self.b0)
-            self.copy(slot, self.peer0, 3 * h - 1 + d).wait_recv()
-            self.copy(slot, self.peer0, 3 * h - 1 + d).start()
+        slot = self.slot(d, self.b1, self.b0)
+        self.copy(slot, self.peer1, h - 1 + d).wait_recv()
+        self.copy(slot, self.peer1, h - 1 + d).start()
+        self.copy(slot, self.peer0, 2 * h - 1 + d).start()
+
+    def third(self, d):
+        slot = self.slot(d, 1 - self.b1, self.b0)
+        self.copy(slot, self.peer0, 3 * self.high - 1 + d).wait_recv()
+        self.copy(slot, self.peer0, 3 * self.high - 1 + d).start()
 
     def finish(self):
         h = self.high
@@ -240,11 +249,13 @@
 
 def kernel(
     n, heads, picked, stride,
-    seg_ref, glob_ref, x_ref, gain1_ref, gain_mlp_ref, gain2_ref,
+    seg_hbm, glob_hbm, x_hbm, gain1_hbm, gain_mlp_hbm, gain2_hbm,
     wq1_hbm, wk1_hbm, wv1_hbm, wo1_hbm, up_hbm, down_hbm, wq2_hbm, wk2_hbm, wv2_hbm, wo2_hbm,
     out_ref,
-    wq1, wk1, wv1, wo1, up, down, wq2, wk2, wv2, wo2, wo_pad1, wo_pad2,
-    xp, q, kv1, kv2, km, vp, perm, perm_back, mix, inner, sem, ssem1, rsem1, ssem2, rsem2,
+    seg_ref, glob_ref, x_ref, gain1_ref, gain_mlp_ref, gain2_ref,
+    wq1, wk1, wv1, wo1, up, down, wq2, wk2, wv2, wo2,
+    xp, q, kva, kvb, kv2, km, vt, perm, perm_back, mix, sem,
+    ssema, rsema, ssemb, rsemb, ssem2, rsem2,
 ):
     tokens, width = x_ref.shape
     size = width // heads
@@ -254,17 +265,22 @@
     keys = n * picked
     group = WINDOW // stride
     scale = size ** -0.5 * math.log2(math.e)
+    side = width // 2
 
     pairs = [(wk1_hbm, wk1), (wv1_hbm, wv1), (wq1_hbm, wq1), (wo1_hbm, wo1), (up_hbm, up),
-             (down_hbm, down), (wk2_hbm, wk2), (wv2_hbm, wv2), (wq2_hbm, wq2), (wo2_hbm, wo2)]
+             (down_hbm, down), (wk2_hbm, wk2), (wv2_hbm, wv2), (wq2_hbm, wq2), (wo2_hbm, wo2),
+             (seg_hbm, seg_ref), (x_hbm, x_ref), (gain1_hbm, gain1_ref), (glob_hbm, glob_ref),
+             (gain_mlp_hbm, gain_mlp_ref), (gain2_hbm, gain2_ref)]
     loads = [pltpu.make_async_copy(a, b, sem.at[i]) for i, (a, b) in enumerate(pairs)]
-    for load in loads:
-        load.start()
-
-    first_gather = Gather(n, kv1, ssem1, rsem1)
+    early = (10, 11, 12, 13, 14, 15, 0, 1)
+    for i in early:
+        loads[i].start()
+
+    gather_a = Gather(n, kva, ssema, rsema)
+    gather_b = Gather(n, kvb, ssemb, rsemb)
     second_gather = Gather(n, kv2, ssem2, rsem2)
     barrier = pltpu.get_barrier_semaphore()
-    peers = first_gather.peers()
+    peers = gather_a.peers()
     for peer in peers:
         pl.semaphore_signal(barrier, inc=1, device_id={"seq": peer}, device_id_type=MESH)
 
@@ -279,17 +295,29 @@
 
     rows = iota((chunk, 1), 0)
     pick = rows % picked
+    loads[10].wait()
     target = pick * stride + head_column(seg_ref, heads, picked)
     onehot = (iota((chunk, tokens), 1) == target).astype(F32).astype(BF16)
+    loads[11].wait()
+    loads[12].wait()
+    for i in range(2, 10):
+        loads[i].start()
     hidden = norm_rows(dot32(onehot, x_ref[...]), gain1_ref[...][None, :])
-    me = first_gather.me
+    me = gather_a.me
     loads[0].wait()
-    kv1[me, 0:picked, :] = own_heads(hidden, wk1)
+    key = own_heads(hidden, wk1)
+    kva[me, 0:picked, :] = key[:, :side]
+    kvb[me, 0:picked, :] = key[:, side:]
     loads[1].wait()
-    kv1[me, picked:2 * picked, :] = own_heads(hidden, wv1)
+    value = own_heads(hidden, wv1)
+    kva[me, picked:2 * picked, :] = value[:, :side]
+    kvb[me, picked:2 * picked, :] = value[:, side:]
     pl.semaphore_wait(barrier, len(peers))
-    first_gather.start()
-
+    gather_a.start()
+    gather_b.start()
+
+    for i in (13, 14, 15):
+        loads[i].wait()
     glob_col = head_column(glob_ref, heads, picked)
     lane = iota((16, WINDOW), 1)
     inside = lane % stride
@@ -323,57 +351,85 @@
 
     for h in range(heads):
         km[h] = jnp.zeros((WINDOW, keys), BF16)
-        i = h % 2
-        ones = iota((keys, LANES), 1) // half == i
-        vp[h // 2, i * keys:(i + 1) * keys, LANES:] = jnp.where(ones, 1.0, 0.0).astype(BF16)
-    for source, padded, load in ((wo1, wo_pad1, loads[3]), (wo2, wo_pad2, None)):
-        if load is None:
-            continue
-        load.wait()
-        for h in range(heads):
-            padded[h * half:h * half + size, :] = source[h * size:(h + 1) * size, :]
-            padded[h * half + size:(h + 1) * half, :] = jnp.zeros((half - size, width), BF16)
-
-    first_gather.second()
+        vt[h * half + size:(h + 1) * half, :] = jnp.ones((half - size, keys), BF16)
 
     loads[2].wait()
+    loads[3].wait()
+    high = gather_a.high
 
     def query_chunk(c, carry):
         at = pl.ds(pl.multiple_of(c * chunk, chunk), chunk)
         hidden = norm_rows(xp[at, :].astype(F32), gain1_ref[...][None, :])
         q[at, :] = dot32(hidden, wq1[...]).astype(BF16)
+        for d in range(1, high):
+            @pl.when(c == d % chunks)
+            def _(d=d):
+                gather_a.second(d)
+
         return carry
 
     lax.fori_loop(0, chunks, query_chunk, 0)
-    first_gather.third()
-    first_gather.finish()
-
-    def set_keys(kv):
-        key = kv[:, 0:picked, :].reshape(keys, width)
-        value = kv[:, picked:2 * picked, :].reshape(keys, width)
-        turned = key.astype(F32).T.astype(BF16)
-        for h in range(heads):
+    gather_a.third(0)
+    gather_b.second(1)
+    for d in range(1, high):
+        gather_a.third(d)
+    for d in range(2, high):
+        gather_b.second(d)
+    gather_a.finish()
+
+    def set_keys(kv, first, last):
+        span = (last - first) * size
+        key = kv[:, 0:picked, :].reshape(keys, span).astype(F32).T.astype(BF16)
+        value = kv[:, picked:2 * picked, :].reshape(keys, span).astype(F32).T.astype(BF16)
+        for h in range(first, last):
             begin = h * size - window_of(h)
-            km[h, begin:begin + size, :] = turned[h * size:(h + 1) * size, :]
-            i = h % 2
-            c, l = iota((WINDOW, LANES), 0) - begin, iota((WINDOW, LANES), 1) - i * half
-            shift = jnp.where((c == l) & (l >= 0) & (l < size), 1.0, 0.0).astype(BF16)
-            moved = dot32(value[:, window_of(h):window_of(h) + WINDOW], shift)
-            vp[h // 2, i * keys:(i + 1) * keys, 0:LANES] = moved.astype(BF16)
-
-    def attend(at):
-        for pair in range(heads // 2):
-            parts = []
-            for h in (2 * pair, 2 * pair + 1):
-                start = window_of(h)
-                scores = dot32(q[at, start:start + WINDOW], km[h])
-                top = jnp.max(scores, axis=-1, keepdims=True)
-                parts.append(jnp.exp2((scores - top) * scale).astype(BF16))
-            both = dot32(jnp.concatenate(parts, axis=1), vp[pair])
-            mixed = both[:, :LANES] / both[:, LANES:]
-            mix[:, pair * LANES:(pair + 1) * LANES] = mixed.astype(BF16)
-
-    set_keys(kv1)
+            at = (h - first) * size
+            km[h, begin:begin + size, :] = key[at:at + size, :]
+            vt[h * half:h * half + size, :] = value[at:at + size, :]
+
+    def attend(c, first, last):
+        at = pl.ds(pl.multiple_of(c * chunk, chunk), chunk)
+
+        def score(h):
+            start = window_of(h)
+            return dot32(q[at, start:start + WINDOW], km[h])
+
+        def soften(scores):
+            top = jnp.max(scores, axis=-1, keepdims=True)
+            return jnp.exp2((scores - top) * scale).astype(BF16)
+
+        def blend(h, weights):
+            both = dot_last(vt[h * half:(h + 1) * half, :], weights)
+            mixed = both[:size] * (1.0 / both[size:size + 1])
+            mix[c, h * size:(h + 1) * size, :] = mixed.astype(BF16)
+
+        steps = (last - first) // GROUP
+        scores, weights = {}, {}
+        for i in range(steps + 2):
+            if i < steps:
+                for h in range(first + i * GROUP, first + (i + 1) * GROUP):
+                    scores[h] = score(h)
+            if 1 <= i <= steps:
+                for h in range(first + (i - 1) * GROUP, first + i * GROUP):
+                    weights[h] = soften(scores.pop(h))
+            if i >= 2:
+                for h in range(first + (i - 2) * GROUP, first + (i - 1) * GROUP):
+                    blend(h, weights.pop(h))
+
+    set_keys(kva, 0, heads // 2)
+
+    def early_chunk(c, carry):
+        attend(c, 0, heads // 2)
+        for d in range(high):
+            @pl.when(c == d % chunks)
+            def _(d=d):
+                gather_b.third(d)
+
+        return carry
+
+    lax.fori_loop(0, chunks, early_chunk, 0)
+    gather_b.finish()
+    set_keys(kvb, heads // 2, heads)
     loads[4].wait()
     loads[5].wait()
     loads[6].wait()
@@ -382,14 +438,19 @@
 
     def first_chunk(c, carry):
         at = pl.ds(pl.multiple_of(c * chunk, chunk), chunk)
-        attend(at)
-        first = (xp[at, :].astype(F32) + dot32(mix[...], wo_pad1[...])).astype(BF16)
-        normed = norm_rows(first.astype(F32), gain_mlp_ref[...][None, :])
-        hidden_units = up.shape[1]
-        for start in range(0, hidden_units, width):
-            part = dot32(normed, up[:, start:start + width])
-            inner[:, start:start + width] = gelu(part).astype(BF16)
-        second = (first.astype(F32) + dot32(inner[...], down[...])).astype(BF16)
+        attend(c, heads // 2, heads)
+        first = (xp[at, :].astype(F32) + dot_first(mix[c], wo1[...])).astype(BF16)
+        total = first.astype(F32)
+        normed = norm_rows(total, gain_mlp_ref[...][None, :])
+        blocks = up.shape[1] // WINDOW
+        units = {}
+        for j in range(blocks + 1):
+            if j < blocks:
+                part = dot32(normed, up[:, j * WINDOW:(j + 1) * WINDOW])
+                units[j] = gelu(part).astype(BF16)
+            if j >= 1:
+                total = total + dot32(units.pop(j - 1), down[(j - 1) * WINDOW:j * WINDOW, :])
+        second = total.astype(BF16)
         xp[at, :] = second
         hidden_two = norm_rows(second.astype(F32), gain2_ref[...][None, :])
         q[at, :] = dot32(hidden_two, wq2[...]).astype(BF16)
@@ -403,26 +464,25 @@
 
         @pl.when(c == 1)
         def _():
-            second_gather.second()
+            for d in range(1, high):
+                second_gather.second(d)
 
         @pl.when(c == 2)
         def _():
-            second_gather.third()
+            for d in range(high):
+                second_gather.third(d)
 
         return carry
 
     lax.fori_loop(0, chunks, first_chunk, 0)
     loads[9].wait()
-    for h in range(heads):
-        wo_pad2[h * half:h * half + size, :] = wo2[h * size:(h + 1) * size, :]
-        wo_pad2[h * half + size:(h + 1) * half, :] = jnp.zeros((half - size, width), BF16)
     second_gather.finish()
-    set_keys(kv2)
+    set_keys(kv2, 0, heads)
 
     def last_chunk(c, carry):
         at = pl.ds(pl.multiple_of(c * chunk, chunk), chunk)
-        attend(at)
-        xp[at, :] = (xp[at, :].astype(F32) + dot32(mix[...], wo_pad2[...])).astype(BF16)
+        attend(c, 0, heads)
+        xp[at, :] = (xp[at, :].astype(F32) + dot_first(mix[c], wo2[...])).astype(BF16)
         return carry
 
     lax.fori_loop(0, chunks, last_chunk, 0)
@@ -448,33 +508,35 @@
     stride = count // picked
     units = up_weight.shape[1]
     chunk = heads * picked
-    any_space = pl.BlockSpec(memory_space=pl.ANY)
+    outside = pl.BlockSpec(memory_space=pltpu.HBM)
     vmem = pl.BlockSpec(memory_space=pltpu.VMEM)
-    smem = pl.BlockSpec(memory_space=pltpu.SMEM)
     square = pltpu.VMEM((width, width), BF16)
-    padded = pltpu.VMEM((heads * LANES // 2, width), BF16)
+    gain = pltpu.VMEM((width,), F32)
+    part = pltpu.VMEM((n, 2 * picked, width // 2), BF16)
+    links = pltpu.SemaphoreType.DMA((n,))
     return pl.pallas_call(
         functools.partial(kernel, n, heads, picked, stride),
         out_shape=jax.ShapeDtypeStruct(tokens.shape, tokens.dtype),
-        in_specs=[smem, smem, vmem, vmem, vmem, vmem] + [any_space] * 10,
+        in_specs=[outside] * 16,
         out_specs=vmem,
         scratch_shapes=[
+            pltpu.SMEM((heads,), jnp.int32), pltpu.SMEM((heads,), jnp.int32),
+            pltpu.VMEM((count, width), BF16),
+            gain, gain, gain,
             square, square, square, square,
             pltpu.VMEM((width, units), BF16), pltpu.VMEM((units, width), BF16),
-            square, square, square, square, padded, padded,
+            square, square, square, square,
             pltpu.VMEM((count, width), BF16),
             pltpu.VMEM((count, width), BF16),
-            pltpu.VMEM((n, 2 * picked, width), BF16),
+            part, part,
             pltpu.VMEM((n, 2 * picked, width), BF16),
             pltpu.VMEM((heads, WINDOW, KEYS), BF16),
-            pltpu.VMEM((heads // 2, 2 * KEYS, 2 * LANES), BF16),
+            pltpu.VMEM((heads * LANES // 2, KEYS), BF16),
             pltpu.VMEM((WINDOW, WINDOW), BF16),
             pltpu.VMEM((WINDOW, WINDOW), BF16),
-            pltpu.VMEM((chunk, heads * LANES // 2), BF16),
-            pltpu.VMEM((chunk, units), BF16),
-            pltpu.SemaphoreType.DMA((10,)),
-            pltpu.SemaphoreType.DMA((n,)), pltpu.SemaphoreType.DMA((n,)),
-            pltpu.SemaphoreType.DMA((n,)), pltpu.SemaphoreType.DMA((n,)),
+            pltpu.VMEM((count // chunk, width, chunk), BF16),
+            pltpu.SemaphoreType.DMA((16,)),
+            links, links, links, links, links, links,
         ],
         compiler_params=pltpu.CompilerParams(
             collective_id=0, has_side_effects=True, vmem_limit_bytes=60 << 20

time: 57.2 us -> 56.7 us (level)
  no operation moved by 1% of the time
where the time goes in v1:
time: 56.7 us; the launch traced here: 56.6 us
  Pallas kernels  53.9 us (95%)
  local copies, waits for them, and re-layouts  2.65 us (5%)
    pallas_call x1, Pallas kernels, whole_body(): pl.pallas_call(functools.partial(kernel, n, heads, picked, stride), out_s...  53.9 us
    unnamed x1, local copies, waits for them, and re-layouts  2.65 us

profile of v1, /device:TPU:0, one launch (start us, length us, event | category | flops | bytes accessed | tf_op | source)
XLA Modules:
  0.0 56.6 jit_solution(4102583828567768455)
XLA Ops:
  0.0 53.9 %encoder.1 = bf16[1024,768]{1,0:T(8,128)(2,1)} custom-call(s32[16]{0:T(128)} %seg_hbm.1, s32[16]{0:T(128)} %glob_hbm.1, bf16[1024,768]{1,0:T(8,128)(2,1)} %x_hbm.1, f32[768]{0:T(1024)} %gain1_hbm.1, f32[768]{0:T(1024)} %gain_mlp_hbm.1, f32[768]{0:T(1024)} %gain2_hbm.1, bf16[768,768]{1,0:T(8,128)(2,1)} %wq1_hbm.1, bf16[768,768]{1,0:T(8,128)(2,1)} %wk1_hbm.1, ...), custom_call_target="tpu_custom_call" | custom-call | tf_op jit(solution)/shard_map/encoder/pallas_call | solution.py:517
  53.9 2.7 %copy.18 = bf16[1024,768]{1,0:T(8,128)(2,1)} copy(bf16[1024,768]{1,0:T(8,128)(2,1)} %encoder.1) | data formatting | bytes 3145728

commit v2 on v1

--- a/solution.py
+++ b/solution.py
@@ -254,8 +254,8 @@
     out_ref,
     seg_ref, glob_ref, x_ref, gain1_ref, gain_mlp_ref, gain2_ref,
     wq1, wk1, wv1, wo1, up, down, wq2, wk2, wv2, wo2,
-    xp, q, kva, kvb, kv2, km, vt, perm, perm_back, mix, sem,
-    ssema, rsema, ssemb, rsemb, ssem2, rsem2,
+    xp, q, kv1, kv2, km, vt, perm, perm_back, mix, mix_odd, sem,
+    ssem1, rsem1, ssem2, rsem2,
 ):
     tokens, width = x_ref.shape
     size = width // heads
@@ -265,7 +265,6 @@
     keys = n * picked
     group = WINDOW // stride
     scale = size ** -0.5 * math.log2(math.e)
-    side = width // 2
 
     pairs = [(wk1_hbm, wk1), (wv1_hbm, wv1), (wq1_hbm, wq1), (wo1_hbm, wo1), (up_hbm, up),
              (down_hbm, down), (wk2_hbm, wk2), (wv2_hbm, wv2), (wq2_hbm, wq2), (wo2_hbm, wo2),
@@ -276,22 +275,26 @@
     for i in early:
         loads[i].start()
 
-    gather_a = Gather(n, kva, ssema, rsema)
-    gather_b = Gather(n, kvb, ssemb, rsemb)
+    first_gather = Gather(n, kv1, ssem1, rsem1)
     second_gather = Gather(n, kv2, ssem2, rsem2)
     barrier = pltpu.get_barrier_semaphore()
-    peers = gather_a.peers()
+    peers = first_gather.peers()
     for peer in peers:
         pl.semaphore_signal(barrier, inc=1, device_id={"seq": peer}, device_id_type=MESH)
 
     def own_heads(hidden, weight):
-        full = dot32(hidden, weight[...])
-        column = iota((picked, width), 1)
-        total = jnp.zeros((picked, width), F32)
-        for h in range(heads):
-            mine = (column >= h * size) & (column < h * size + size)
-            total = jnp.where(mine, full[h * picked:(h + 1) * picked], total)
-        return total.astype(BF16)
+        blocks = []
+        for start in range(0, width, WINDOW):
+            low, top = start // size, -(-(start + WINDOW) // size)
+            full = dot32(hidden[low * picked:top * picked], weight[:, start:start + WINDOW])
+            column = iota((picked, WINDOW), 1) + start
+            total = jnp.zeros((picked, WINDOW), F32)
+            for h in range(low, top):
+                mine = (column >= h * size) & (column < h * size + size)
+                at = (h - low) * picked
+                total = jnp.where(mine, full[at:at + picked], total)
+            blocks.append(total)
+        return jnp.concatenate(blocks, axis=1).astype(BF16)
 
     rows = iota((chunk, 1), 0)
     pick = rows % picked
@@ -303,18 +306,13 @@
     for i in range(2, 10):
         loads[i].start()
     hidden = norm_rows(dot32(onehot, x_ref[...]), gain1_ref[...][None, :])
-    me = gather_a.me
+    me = first_gather.me
     loads[0].wait()
-    key = own_heads(hidden, wk1)
-    kva[me, 0:picked, :] = key[:, :side]
-    kvb[me, 0:picked, :] = key[:, side:]
+    kv1[me, 0:picked, :] = own_heads(hidden, wk1)
     loads[1].wait()
-    value = own_heads(hidden, wv1)
-    kva[me, picked:2 * picked, :] = value[:, :side]
-    kvb[me, picked:2 * picked, :] = value[:, side:]
+    kv1[me, picked:2 * picked, :] = own_heads(hidden, wv1)
     pl.semaphore_wait(barrier, len(peers))
-    gather_a.start()
-    gather_b.start()
+    first_gather.start()
 
     for i in (13, 14, 15):
         loads[i].wait()
@@ -355,27 +353,23 @@
 
     loads[2].wait()
     loads[3].wait()
-    high = gather_a.high
+    high = first_gather.high
 
     def query_chunk(c, carry):
         at = pl.ds(pl.multiple_of(c * chunk, chunk), chunk)
         hidden = norm_rows(xp[at, :].astype(F32), gain1_ref[...][None, :])
         q[at, :] = dot32(hidden, wq1[...]).astype(BF16)
         for d in range(1, high):
-            @pl.when(c == d % chunks)
+            @pl.when(c == d - 1)
             def _(d=d):
-                gather_a.second(d)
+                first_gather.second(d)
 
         return carry
 
     lax.fori_loop(0, chunks, query_chunk, 0)
-    gather_a.third(0)
-    gather_b.second(1)
-    for d in range(1, high):
-        gather_a.third(d)
-    for d in range(2, high):
-        gather_b.second(d)
-    gather_a.finish()
+    for d in range(high):
+        first_gather.third(d)
+    first_gather.finish()
 
     def set_keys(kv, first, last):
         span = (last - first) * size
@@ -387,9 +381,7 @@
             km[h, begin:begin + size, :] = key[at:at + size, :]
             vt[h * half:h * half + size, :] = value[at:at + size, :]
 
-    def attend(c, first, last):
-        at = pl.ds(pl.multiple_of(c * chunk, chunk), chunk)
-
+    def attend(at, mix):
         def score(h):
             start = window_of(h)
             return dot32(q[at, start:start + WINDOW], km[h])
@@ -401,59 +393,61 @@
         def blend(h, weights):
             both = dot_last(vt[h * half:(h + 1) * half, :], weights)
             mixed = both[:size] * (1.0 / both[size:size + 1])
-            mix[c, h * size:(h + 1) * size, :] = mixed.astype(BF16)
-
-        steps = (last - first) // GROUP
+            mix[h * size:(h + 1) * size, :] = mixed.astype(BF16)
+
+        steps = heads // GROUP
         scores, weights = {}, {}
         for i in range(steps + 2):
             if i < steps:
-                for h in range(first + i * GROUP, first + (i + 1) * GROUP):
+                for h in range(i * GROUP, (i + 1) * GROUP):
                     scores[h] = score(h)
             if 1 <= i <= steps:
-                for h in range(first + (i - 1) * GROUP, first + i * GROUP):
+                for h in range((i - 1) * GROUP, i * GROUP):
                     weights[h] = soften(scores.pop(h))
             if i >= 2:
-                for h in range(first + (i - 2) * GROUP, first + (i - 1) * GROUP):
+                for h in range((i - 2) * GROUP, (i - 1) * GROUP):
                     blend(h, weights.pop(h))
-
-    set_keys(kva, 0, heads // 2)
-
-    def early_chunk(c, carry):
-        attend(c, 0, heads // 2)
-        for d in range(high):
-            @pl.when(c == d % chunks)
-            def _(d=d):
-                gather_b.third(d)
-
-        return carry
-
-    lax.fori_loop(0, chunks, early_chunk, 0)
-    gather_b.finish()
-    set_keys(kvb, heads // 2, heads)
+            yield i
+
+    def rows_of(c):
+        return pl.ds(pl.multiple_of(c * chunk, chunk), chunk)
+
+    set_keys(kv1, 0, heads)
     loads[4].wait()
     loads[5].wait()
     loads[6].wait()
     loads[7].wait()
     loads[8].wait()
 
-    def first_chunk(c, carry):
-        at = pl.ds(pl.multiple_of(c * chunk, chunk), chunk)
-        attend(c, heads // 2, heads)
-        first = (xp[at, :].astype(F32) + dot_first(mix[c], wo1[...])).astype(BF16)
+    for _ in attend(rows_of(0), mix):
+        pass
+
+    def first_chunk(c, more):
+        at = rows_of(c)
+        first = (xp[at, :].astype(F32) + dot_first(mix[...], wo1[...])).astype(BF16)
         total = first.astype(F32)
         normed = norm_rows(total, gain_mlp_ref[...][None, :])
         blocks = up.shape[1] // WINDOW
         units = {}
+        ahead = attend(rows_of(c + 1), mix) if more else iter(())
         for j in range(blocks + 1):
+            next(ahead, None)
             if j < blocks:
                 part = dot32(normed, up[:, j * WINDOW:(j + 1) * WINDOW])
                 units[j] = gelu(part).astype(BF16)
             if j >= 1:
                 total = total + dot32(units.pop(j - 1), down[(j - 1) * WINDOW:j * WINDOW, :])
+        for _ in ahead:
+            pass
         second = total.astype(BF16)
         xp[at, :] = second
         hidden_two = norm_rows(second.astype(F32), gain2_ref[...][None, :])
         q[at, :] = dot32(hidden_two, wq2[...]).astype(BF16)
+
+        return hidden_two
+
+    def first_step(c, carry):
+        hidden_two = first_chunk(c, True)
 
         @pl.when(c == 0)
         def _():
@@ -474,18 +468,31 @@
 
         return carry
 
-    lax.fori_loop(0, chunks, first_chunk, 0)
+    lax.fori_loop(0, chunks - 1, first_step, 0)
+    first_chunk(chunks - 1, False)
     loads[9].wait()
     second_gather.finish()
     set_keys(kv2, 0, heads)
 
-    def last_chunk(c, carry):
-        at = pl.ds(pl.multiple_of(c * chunk, chunk), chunk)
-        attend(c, 0, heads)
-        xp[at, :] = (xp[at, :].astype(F32) + dot_first(mix[c], wo2[...])).astype(BF16)
-        return carry
-
-    lax.fori_loop(0, chunks, last_chunk, 0)
+    def project(c):
+        at = rows_of(c)
+        for start in range(0, width, WINDOW):
+            part = dot_first(mixes[c % 2][...], wo2[:, start:start + WINDOW])
+            column = slice(start, start + WINDOW)
+            xp[at, column] = (xp[at, column].astype(F32) + part).astype(BF16)
+            yield start
+
+    mixes = (mix, mix_odd)
+    behind = iter(())
+    for c in range(chunks):
+        for i in attend(rows_of(c), mixes[c % 2]):
+            if i >= 1:
+                next(behind, None)
+        for _ in behind:
+            pass
+        behind = project(c)
+    for _ in behind:
+        pass
     for g in range(tokens // WINDOW):
         blocks = []
         for j in range(group):
@@ -512,7 +519,7 @@
     vmem = pl.BlockSpec(memory_space=pltpu.VMEM)
     square = pltpu.VMEM((width, width), BF16)
     gain = pltpu.VMEM((width,), F32)
-    part = pltpu.VMEM((n, 2 * picked, width // 2), BF16)
+    shared = pltpu.VMEM((n, 2 * picked, width), BF16)
     links = pltpu.SemaphoreType.DMA((n,))
     return pl.pallas_call(
         functools.partial(kernel, n, heads, picked, stride),
@@ -528,15 +535,15 @@
             square, square, square, square,
             pltpu.VMEM((count, width), BF16),
             pltpu.VMEM((count, width), BF16),
-            part, part,
-            pltpu.VMEM((n, 2 * picked, width), BF16),
+            shared, shared,
             pltpu.VMEM((heads, WINDOW, KEYS), BF16),
             pltpu.VMEM((heads * LANES // 2, KEYS), BF16),
             pltpu.VMEM((WINDOW, WINDOW), BF16),
             pltpu.VMEM((WINDOW, WINDOW), BF16),
-            pltpu.VMEM((count // chunk, width, chunk), BF16),
+            pltpu.VMEM((width, chunk), BF16),
+            pltpu.VMEM((width, chunk), BF16),
             pltpu.SemaphoreType.DMA((16,)),
-            links, links, links, links, links, links,
+            links, links, links, links,
         ],
         compiler_params=pltpu.CompilerParams(
             collective_id=0, has_side_effects=True, vmem_limit_bytes=60 << 20

time: 56.7 us -> 51.7 us (0.912)
  Pallas kernels: 53.9 us -> 48.9 us
    pallas_call x1, Pallas kernels: 53.9 us -> 48.9 us  [whole_body(): pl.pallas_call(functools.partial(kernel, n, heads, picked, stride), out_s...]
where the time goes in v2:
time: 51.7 us; the launch traced here: 51.6 us
  Pallas kernels  48.9 us (95%)
  local copies, waits for them, and re-layouts  2.65 us (5%)
    pallas_call x1, Pallas kernels, whole_body(): pl.pallas_call(functools.partial(kernel, n, heads, picked, stride), out_s...  48.9 us
    unnamed x1, local copies, waits for them, and re-layouts  2.65 us

profile of v2, /device:TPU:0, one launch (start us, length us, event | category | flops | bytes accessed | tf_op | source)
XLA Modules:
  0.0 51.6 jit_solution(12148357088645872246)
XLA Ops:
  0.0 48.9 %encoder.1 = bf16[1024,768]{1,0:T(8,128)(2,1)} custom-call(s32[16]{0:T(128)} %seg_hbm.1, s32[16]{0:T(128)} %glob_hbm.1, bf16[1024,768]{1,0:T(8,128)(2,1)} %x_hbm.1, f32[768]{0:T(1024)} %gain1_hbm.1, f32[768]{0:T(1024)} %gain_mlp_hbm.1, f32[768]{0:T(1024)} %gain2_hbm.1, bf16[768,768]{1,0:T(8,128)(2,1)} %wq1_hbm.1, bf16[768,768]{1,0:T(8,128)(2,1)} %wk1_hbm.1, ...), custom_call_target="tpu_custom_call" | custom-call | tf_op jit(solution)/shard_map/encoder/pallas_call | solution.py:524
  48.9 2.7 %copy.18 = bf16[1024,768]{1,0:T(8,128)(2,1)} copy(bf16[1024,768]{1,0:T(8,128)(2,1)} %encoder.1) | data formatting | bytes 3145728

commit v3 on v2

--- a/solution.py
+++ b/solution.py
@@ -205,6 +205,9 @@
             device_id_type=MESH,
         )
 
+    def far(self, d):
+        return ((self.hi + d) % self.high) * 4 + self.b1 * 2 + self.b0
+
     def peers(self):
         out = [((self.hi + d) % self.high) * 4 + self.b1 * 2 + self.b0 for d in range(1, self.high)]
         return out + [self.peer1, self.peer0]
@@ -223,6 +226,24 @@
         self.copy(slot, self.peer1, h - 1 + d).wait_recv()
         self.copy(slot, self.peer1, h - 1 + d).start()
         self.copy(slot, self.peer0, 2 * h - 1 + d).start()
+
+    def start_across(self):
+        self.copy(self.me, self.peer1, 0).start()
+        self.copy(self.me, self.peer0, 1).start()
+        for d in range(1, self.high):
+            self.copy(self.me, self.far(d), 1 + d).start()
+
+    def turn(self):
+        slot = self.peer1
+        self.copy(slot, self.peer0, 2 * self.high).wait_recv()
+        for d in range(1, self.high):
+            self.copy(slot, self.far(d), self.high + d).start()
+        self.copy(slot, self.peer0, 2 * self.high).start()
+
+    def relay(self, d, b1, k):
+        slot = self.slot(d, b1, self.b0)
+        self.copy(slot, self.peer0, k).wait_recv()
+        self.copy(slot, self.peer0, k).start()
 
     def third(self, d):
         slot = self.slot(d, 1 - self.b1, self.b0)
@@ -254,8 +275,8 @@
     out_ref,
     seg_ref, glob_ref, x_ref, gain1_ref, gain_mlp_ref, gain2_ref,
     wq1, wk1, wv1, wo1, up, down, wq2, wk2, wv2, wo2,
-    xp, q, kv1, kv2, km, vt, perm, perm_back, mix, mix_odd, sem,
-    ssem1, rsem1, ssem2, rsem2,
+    xp, q, q_two, normed, key1, value1, kv2, km, vt, perm, perm_back, mix, mix_odd, sem,
+    ssemk, rsemk, ssemv, rsemv, ssem2, rsem2,
 ):
     tokens, width = x_ref.shape
     size = width // heads
@@ -275,10 +296,11 @@
     for i in early:
         loads[i].start()
 
-    first_gather = Gather(n, kv1, ssem1, rsem1)
+    key_gather = Gather(n, key1, ssemk, rsemk)
+    value_gather = Gather(n, value1, ssemv, rsemv)
     second_gather = Gather(n, kv2, ssem2, rsem2)
     barrier = pltpu.get_barrier_semaphore()
-    peers = first_gather.peers()
+    peers = key_gather.peers()
     for peer in peers:
         pl.semaphore_signal(barrier, inc=1, device_id={"seq": peer}, device_id_type=MESH)
 
@@ -306,13 +328,14 @@
     for i in range(2, 10):
         loads[i].start()
     hidden = norm_rows(dot32(onehot, x_ref[...]), gain1_ref[...][None, :])
-    me = first_gather.me
+    me = key_gather.me
     loads[0].wait()
-    kv1[me, 0:picked, :] = own_heads(hidden, wk1)
+    key1[me] = own_heads(hidden, wk1)
+    pl.semaphore_wait(barrier, len(peers))
+    key_gather.start()
     loads[1].wait()
-    kv1[me, picked:2 * picked, :] = own_heads(hidden, wv1)
-    pl.semaphore_wait(barrier, len(peers))
-    first_gather.start()
+    value1[me] = own_heads(hidden, wv1)
+    value_gather.start_across()
 
     for i in (13, 14, 15):
         loads[i].wait()
@@ -353,35 +376,43 @@
 
     loads[2].wait()
     loads[3].wait()
-    high = first_gather.high
+    high = key_gather.high
 
     def query_chunk(c, carry):
         at = pl.ds(pl.multiple_of(c * chunk, chunk), chunk)
         hidden = norm_rows(xp[at, :].astype(F32), gain1_ref[...][None, :])
         q[at, :] = dot32(hidden, wq1[...]).astype(BF16)
+        @pl.when(c == 0)
+        def _():
+            value_gather.turn()
+
         for d in range(1, high):
-            @pl.when(c == d - 1)
+            @pl.when(c == d)
             def _(d=d):
-                first_gather.second(d)
+                key_gather.second(d)
 
         return carry
 
     lax.fori_loop(0, chunks, query_chunk, 0)
-    for d in range(high):
-        first_gather.third(d)
-    first_gather.finish()
-
-    def set_keys(kv, first, last):
-        span = (last - first) * size
-        key = kv[:, 0:picked, :].reshape(keys, span).astype(F32).T.astype(BF16)
-        value = kv[:, picked:2 * picked, :].reshape(keys, span).astype(F32).T.astype(BF16)
-        for h in range(first, last):
+    key_gather.third(0)
+    for d in range(1, high):
+        value_gather.relay(d, value_gather.b1, 2 * high + d)
+        key_gather.third(d)
+    for d in range(1, high):
+        value_gather.relay(d, 1 - value_gather.b1, 3 * high - 1 + d)
+    key_gather.finish()
+    value_gather.finish()
+
+    def set_keys(key, value):
+        key = key.reshape(keys, width).astype(F32).T.astype(BF16)
+        value = value.reshape(keys, width).astype(F32).T.astype(BF16)
+        for h in range(heads):
             begin = h * size - window_of(h)
-            at = (h - first) * size
+            at = h * size
             km[h, begin:begin + size, :] = key[at:at + size, :]
             vt[h * half:h * half + size, :] = value[at:at + size, :]
 
-    def attend(at, mix):
+    def attend(at, q, mix):
         def score(h):
             start = window_of(h)
             return dot32(q[at, start:start + WINDOW], km[h])
@@ -412,46 +443,70 @@
     def rows_of(c):
         return pl.ds(pl.multiple_of(c * chunk, chunk), chunk)
 
-    set_keys(kv1, 0, heads)
+    set_keys(key1[...], value1[...])
     loads[4].wait()
     loads[5].wait()
     loads[6].wait()
     loads[7].wait()
     loads[8].wait()
 
-    for _ in attend(rows_of(0), mix):
-        pass
-
-    def first_chunk(c, more):
+    def query_two(c):
         at = rows_of(c)
-        first = (xp[at, :].astype(F32) + dot_first(mix[...], wo1[...])).astype(BF16)
-        total = first.astype(F32)
-        normed = norm_rows(total, gain_mlp_ref[...][None, :])
+        hidden_two = norm_rows(xp[at, :].astype(F32), gain2_ref[...][None, :])
+        for start in range(0, width, WINDOW):
+            column = slice(start, start + WINDOW)
+            q_two[at, column] = dot32(hidden_two, wq2[:, column]).astype(BF16)
+            yield start
+
+    def enter(c):
+        at = rows_of(c)
+        parts = []
+        for start in range(0, width, WINDOW):
+            column = slice(start, start + WINDOW)
+            parts.append(xp[at, column].astype(F32) + dot_first(mix[...], wo1[:, column]))
+            yield start
+        first = jnp.concatenate(parts, axis=1).astype(BF16)
+        xp[at, :] = first
+        normed[...] = norm_rows(first.astype(F32), gain_mlp_ref[...][None, :])
+
+    def first_chunk(c, more, late):
+        at = rows_of(c)
+        total = xp[at, :].astype(F32)
         blocks = up.shape[1] // WINDOW
         units = {}
-        ahead = attend(rows_of(c + 1), mix) if more else iter(())
+        ahead = attend(rows_of(c + 1), q, mix) if more else iter(())
+        behind = query_two(late)
         for j in range(blocks + 1):
             next(ahead, None)
+            if j % 3 == 1:
+                next(behind, None)
             if j < blocks:
-                part = dot32(normed, up[:, j * WINDOW:(j + 1) * WINDOW])
+                part = dot32(normed[...], up[:, j * WINDOW:(j + 1) * WINDOW])
                 units[j] = gelu(part).astype(BF16)
             if j >= 1:
                 total = total + dot32(units.pop(j - 1), down[(j - 1) * WINDOW:j * WINDOW, :])
-        for _ in ahead:
-            pass
+        for rest in (behind, ahead):
+            for _ in rest:
+                pass
         second = total.astype(BF16)
         xp[at, :] = second
-        hidden_two = norm_rows(second.astype(F32), gain2_ref[...][None, :])
-        q[at, :] = dot32(hidden_two, wq2[...]).astype(BF16)
-
-        return hidden_two
+        if more:
+            for _ in enter(c + 1):
+                pass
+        return second
+
+    for _ in attend(rows_of(0), q, mix):
+        pass
+    for _ in enter(0):
+        pass
 
     def first_step(c, carry):
-        hidden_two = first_chunk(c, True)
+        second = first_chunk(c, True, (c + chunks - 1) % chunks)
 
         @pl.when(c == 0)
         def _():
-            picked_rows = dot32(onehot_two, hidden_two).astype(BF16)
+            rows = dot32(onehot_two, second)
+            picked_rows = norm_rows(rows, gain2_ref[...][None, :])
             kv2[me, 0:picked, :] = own_heads(picked_rows, wk2)
             kv2[me, picked:2 * picked, :] = own_heads(picked_rows, wv2)
             second_gather.start()
@@ -469,10 +524,12 @@
         return carry
 
     lax.fori_loop(0, chunks - 1, first_step, 0)
-    first_chunk(chunks - 1, False)
+    first_chunk(chunks - 1, False, chunks - 2)
+    for _ in query_two(chunks - 1):
+        pass
     loads[9].wait()
     second_gather.finish()
-    set_keys(kv2, 0, heads)
+    set_keys(kv2[:, 0:picked, :], kv2[:, picked:2 * picked, :])
 
     def project(c):
         at = rows_of(c)
@@ -485,7 +542,7 @@
     mixes = (mix, mix_odd)
     behind = iter(())
     for c in range(chunks):
-        for i in attend(rows_of(c), mixes[c % 2]):
+        for i in attend(rows_of(c), q_two, mixes[c % 2]):
             if i >= 1:
                 next(behind, None)
         for _ in behind:
@@ -519,7 +576,7 @@
     vmem = pl.BlockSpec(memory_space=pltpu.VMEM)
     square = pltpu.VMEM((width, width), BF16)
     gain = pltpu.VMEM((width,), F32)
-    shared = pltpu.VMEM((n, 2 * picked, width), BF16)
+    own = pltpu.VMEM((n, picked, width), BF16)
     links = pltpu.SemaphoreType.DMA((n,))
     return pl.pallas_call(
         functools.partial(kernel, n, heads, picked, stride),
@@ -535,7 +592,10 @@
             square, square, square, square,
             pltpu.VMEM((count, width), BF16),
             pltpu.VMEM((count, width), BF16),
-            shared, shared,
+            pltpu.VMEM((count, width), BF16),
+            pltpu.VMEM((chunk, width), BF16),
+            own, own,
+            pltpu.VMEM((n, 2 * picked, width), BF16),
             pltpu.VMEM((heads, WINDOW, KEYS), BF16),
             pltpu.VMEM((heads * LANES // 2, KEYS), BF16),
             pltpu.VMEM((WINDOW, WINDOW), BF16),
@@ -543,7 +603,7 @@
             pltpu.VMEM((width, chunk), BF16),
             pltpu.VMEM((width, chunk), BF16),
             pltpu.SemaphoreType.DMA((16,)),
-            links, links, links, links,
+            links, links, links, links, links, links,
         ],
         compiler_params=pltpu.CompilerParams(
             collective_id=0, has_side_effects=True, vmem_limit_bytes=60 << 20

time: 51.7 us -> 49.8 us (0.963)
  Pallas kernels: 48.9 us -> 47 us
    pallas_call x1, Pallas kernels: 48.9 us -> 47 us  [whole_body(): pl.pallas_call(functools.partial(kernel, n, heads, picked, stride), out_s...]
where the time goes in v3:
time: 49.8 us; the launch traced here: 49.7 us
  Pallas kernels  47 us (94%)
  local copies, waits for them, and re-layouts  2.65 us (5%)
    pallas_call x1, Pallas kernels, whole_body(): pl.pallas_call(functools.partial(kernel, n, heads, picked, stride), out_s...  47 us
    unnamed x1, local copies, waits for them, and re-layouts  2.65 us

profile of v3, /device:TPU:0, one launch (start us, length us, event | category | flops | bytes accessed | tf_op | source)
XLA Modules:
  0.0 49.7 jit_solution(955101784222340297)
XLA Ops:
  0.0 47.0 %encoder.1 = bf16[1024,768]{1,0:T(8,128)(2,1)} custom-call(s32[16]{0:T(128)} %seg_hbm.1, s32[16]{0:T(128)} %glob_hbm.1, bf16[1024,768]{1,0:T(8,128)(2,1)} %x_hbm.1, f32[768]{0:T(1024)} %gain1_hbm.1, f32[768]{0:T(1024)} %gain_mlp_hbm.1, f32[768]{0:T(1024)} %gain2_hbm.1, bf16[768,768]{1,0:T(8,128)(2,1)} %wq1_hbm.1, bf16[768,768]{1,0:T(8,128)(2,1)} %wk1_hbm.1, ...), custom_call_target="tpu_custom_call" | custom-call | tf_op jit(solution)/shard_map/encoder/pallas_call | solution.py:581
  47.0 2.7 %copy.18 = bf16[1024,768]{1,0:T(8,128)(2,1)} copy(bf16[1024,768]{1,0:T(8,128)(2,1)} %encoder.1) | data formatting | bytes 3145728

commit v4 on v3

--- a/solution.py
+++ b/solution.py
@@ -272,7 +272,7 @@
     n, heads, picked, stride,
     seg_hbm, glob_hbm, x_hbm, gain1_hbm, gain_mlp_hbm, gain2_hbm,
     wq1_hbm, wk1_hbm, wv1_hbm, wo1_hbm, up_hbm, down_hbm, wq2_hbm, wk2_hbm, wv2_hbm, wo2_hbm,
-    out_ref,
+    out_hbm,
     seg_ref, glob_ref, x_ref, gain1_ref, gain_mlp_ref, gain2_ref,
     wq1, wk1, wv1, wo1, up, down, wq2, wk2, wv2, wo2,
     xp, q, q_two, normed, key1, value1, kv2, km, vt, perm, perm_back, mix, mix_odd, sem,
@@ -382,7 +382,7 @@
         at = pl.ds(pl.multiple_of(c * chunk, chunk), chunk)
         hidden = norm_rows(xp[at, :].astype(F32), gain1_ref[...][None, :])
         q[at, :] = dot32(hidden, wq1[...]).astype(BF16)
-        @pl.when(c == 0)
+        @pl.when(c == 1)
         def _():
             value_gather.turn()
 
@@ -404,6 +404,10 @@
     value_gather.finish()
 
     def set_keys(key, value):
+        for _ in place_keys(key, value):
+            pass
+
+    def place_keys(key, value):
         key = key.reshape(keys, width).astype(F32).T.astype(BF16)
         value = value.reshape(keys, width).astype(F32).T.astype(BF16)
         for h in range(heads):
@@ -411,6 +415,8 @@
             at = h * size
             km[h, begin:begin + size, :] = key[at:at + size, :]
             vt[h * half:h * half + size, :] = value[at:at + size, :]
+            if h % GROUP == 1:
+                yield h
 
     def attend(at, q, mix):
         def score(h):
@@ -477,6 +483,9 @@
         ahead = attend(rows_of(c + 1), q, mix) if more else iter(())
         behind = query_two(late)
         for j in range(blocks + 1):
+            if not more and j == blocks // 4:
+                second_gather.finish()
+                ahead = place_keys(kv2[:, 0:picked, :], kv2[:, picked:2 * picked, :])
             next(ahead, None)
             if j % 3 == 1:
                 next(behind, None)
@@ -525,11 +534,7 @@
 
     lax.fori_loop(0, chunks - 1, first_step, 0)
     first_chunk(chunks - 1, False, chunks - 2)
-    for _ in query_two(chunks - 1):
-        pass
     loads[9].wait()
-    second_gather.finish()
-    set_keys(kv2[:, 0:picked, :], kv2[:, picked:2 * picked, :])
 
     def project(c):
         at = rows_of(c)
@@ -540,7 +545,7 @@
             yield start
 
     mixes = (mix, mix_odd)
-    behind = iter(())
+    behind = query_two(chunks - 1)
     for c in range(chunks):
         for i in attend(rows_of(c), q_two, mixes[c % 2]):
             if i >= 1:
@@ -550,6 +555,7 @@
         behind = project(c)
     for _ in behind:
         pass
+    stores = []
     for g in range(tokens // WINDOW):
         blocks = []
         for j in range(group):
@@ -557,7 +563,12 @@
                 at = c * chunk + (g * group + j) * heads
                 blocks.append(xp[at:at + heads, :])
         moved = dot32(perm_back[...], jnp.concatenate(blocks, axis=0))
-        out_ref[g * WINDOW:(g + 1) * WINDOW, :] = moved.astype(BF16)
+        at = slice(g * WINDOW, (g + 1) * WINDOW)
+        x_ref[at, :] = moved.astype(BF16)
+        stores.append(pltpu.make_async_copy(x_ref.at[at], out_hbm.at[at], sem.at[g]))
+        stores[-1].start()
+    for store in stores:
+        store.wait()
 
 
 def whole_body(
@@ -573,7 +584,6 @@
     units = up_weight.shape[1]
     chunk = heads * picked
     outside = pl.BlockSpec(memory_space=pltpu.HBM)
-    vmem = pl.BlockSpec(memory_space=pltpu.VMEM)
     square = pltpu.VMEM((width, width), BF16)
     gain = pltpu.VMEM((width,), F32)
     own = pltpu.VMEM((n, picked, width), BF16)
@@ -582,7 +592,7 @@
         functools.partial(kernel, n, heads, picked, stride),
         out_shape=jax.ShapeDtypeStruct(tokens.shape, tokens.dtype),
         in_specs=[outside] * 16,
-        out_specs=vmem,
+        out_specs=outside,
         scratch_shapes=[
             pltpu.SMEM((heads,), jnp.int32), pltpu.SMEM((heads,), jnp.int32),
             pltpu.VMEM((count, width), BF16),

time: 49.8 us -> 49.2 us (0.988)
  Pallas kernels: 47 us -> 46.4 us
    pallas_call x1, Pallas kernels: 47 us -> 46.4 us  [whole_body(): pl.pallas_call(functools.partial(kernel, n, heads, picked, stride), out_s...]
where the time goes in v4:
time: 49.2 us; the launch traced here: 49.1 us
  Pallas kernels  46.4 us (94%)
  local copies, waits for them, and re-layouts  2.65 us (5%)
    pallas_call x1, Pallas kernels, whole_body(): pl.pallas_call(functools.partial(kernel, n, heads, picked, stride), out_s...  46.4 us
    unnamed x1, local copies, waits for them, and re-layouts  2.65 us

profile of v4, /device:TPU:0, one launch (start us, length us, event | category | flops | bytes accessed | tf_op | source)
XLA Modules:
  0.0 49.1 jit_solution(6152771808952190706)
XLA Ops:
  0.0 46.4 %encoder.1 = bf16[1024,768]{1,0:T(8,128)(2,1)} custom-call(s32[16]{0:T(128)} %seg_hbm.1, s32[16]{0:T(128)} %glob_hbm.1, bf16[1024,768]{1,0:T(8,128)(2,1)} %x_hbm.1, f32[768]{0:T(1024)} %gain1_hbm.1, f32[768]{0:T(1024)} %gain_mlp_hbm.1, f32[768]{0:T(1024)} %gain2_hbm.1, bf16[768,768]{1,0:T(8,128)(2,1)} %wq1_hbm.1, bf16[768,768]{1,0:T(8,128)(2,1)} %wk1_hbm.1, ...), custom_call_target="tpu_custom_call" | custom-call | tf_op jit(solution)/shard_map/encoder/pallas_call | solution.py:591
  46.4 2.7 %copy.18 = bf16[1024,768]{1,0:T(8,128)(2,1)} copy(bf16[1024,768]{1,0:T(8,128)(2,1)} %encoder.1) | data formatting | bytes 3145728

commit v5 on v4

--- a/solution.py
+++ b/solution.py
@@ -482,6 +482,8 @@
         units = {}
         ahead = attend(rows_of(c + 1), q, mix) if more else iter(())
         behind = query_two(late)
+        entering = enter(c + 1) if more else iter(())
+        done = heads // GROUP + 2
         for j in range(blocks + 1):
             if not more and j == blocks // 4:
                 second_gather.finish()
@@ -489,6 +491,8 @@
             next(ahead, None)
             if j % 3 == 1:
                 next(behind, None)
+            if j >= done:
+                next(entering, None)
             if j < blocks:
                 part = dot32(normed[...], up[:, j * WINDOW:(j + 1) * WINDOW])
                 units[j] = gelu(part).astype(BF16)
@@ -499,9 +503,8 @@
                 pass
         second = total.astype(BF16)
         xp[at, :] = second
-        if more:
-            for _ in enter(c + 1):
-                pass
+        for _ in entering:
+            pass
         return second
 
     for _ in attend(rows_of(0), q, mix):

time: 49.2 us -> 49.1 us (level)
  no operation moved by 1% of the time
where the time goes in v5:
time: 49.1 us; the launch traced here: 49 us
  Pallas kernels  46.3 us (94%)
  local copies, waits for them, and re-layouts  2.65 us (5%)
    pallas_call x1, Pallas kernels, whole_body(): pl.pallas_call(functools.partial(kernel, n, heads, picked, stride), out_s...  46.3 us
    unnamed x1, local copies, waits for them, and re-layouts  2.65 us

profile of v5, /device:TPU:0, one launch (start us, length us, event | category | flops | bytes accessed | tf_op | source)
XLA Modules:
  0.0 49.0 jit_solution(17788614659758942830)
XLA Ops:
  0.0 46.3 %encoder.1 = bf16[1024,768]{1,0:T(8,128)(2,1)} custom-call(s32[16]{0:T(128)} %seg_hbm.1, s32[16]{0:T(128)} %glob_hbm.1, bf16[1024,768]{1,0:T(8,128)(2,1)} %x_hbm.1, f32[768]{0:T(1024)} %gain1_hbm.1, f32[768]{0:T(1024)} %gain_mlp_hbm.1, f32[768]{0:T(1024)} %gain2_hbm.1, bf16[768,768]{1,0:T(8,128)(2,1)} %wq1_hbm.1, bf16[768,768]{1,0:T(8,128)(2,1)} %wk1_hbm.1, ...), custom_call_target="tpu_custom_call" | custom-call | tf_op jit(solution)/shard_map/encoder/pallas_call | solution.py:594
  46.3 2.7 %copy.18 = bf16[1024,768]{1,0:T(8,128)(2,1)} copy(bf16[1024,768]{1,0:T(8,128)(2,1)} %encoder.1) | data formatting | bytes 3145728
